TPU v7x, 32 devices: a whole 2x2x4 slice. The times are simulated.
32 devices in a mesh: league: 4 (over x, core), env: 8 (over z, y).
Axes of the slice: x: 2, y: 2, z: 4, core: 2. Of those that a mesh axis runs over, the one named last changes fastest.
Arguments:
- obs_own: bfloat16 [4, 2, 128, 16, 2048], P('league', None, 'env'), may hold values from -6 to 6
- obs_opp: bfloat16 [4, 2, 128, 16, 2048], P('league', None, 'env'), may hold values from -6 to 6
- actions: int32 [4, 2, 2, 128, 16], P('league', None, None, 'env'), may hold values from 0 to 255
- opponent_picks: int32 [4, 2], P('league'), may hold values from 0 to 3
- policy_weight: bfloat16 [4, 2048, 2048], P('league', 'env'), may hold values from -0.125 to 0.125
- policy_gain: bfloat16 [4, 2048], P('league'), may hold values from 0.25 to 1.75
- action_table: bfloat16 [256, 2048], replicated, may hold values from -6 to 6
- value_gain: bfloat16 [2048], replicated, may hold values from 0.25 to 1.75
- value_up: bfloat16 [2048, 1024], replicated, may hold values from -0.125 to 0.125
- value_out: bfloat16 [1024], replicated, may hold values from -0.1875 to 0.1875
Outputs:
- learner_rows: bfloat16 [4, 2, 16, 2048, 128], P('league', None, None, 'env')
- values: float32 [4, 2, 128, 16], P('league', None, 'env')
All inputs are finite; a program needn't handle non-finite values.
Results may differ from a plain program's by a relative error of at most 0.0054.
Values may be sent and summed in bfloat16 or wider, within the bound.
A program may use at most 128 MiB of HBM per device.

v0:
```python
import jax
import jax.numpy as jnp
from jax import lax
from jax.sharding import PartitionSpec as P


def rms_norm(inputs, gain):
    scale = lax.rsqrt(jnp.mean(inputs * inputs, axis=-1, keepdims=True) + 1e-05)
    return inputs * scale * gain.astype(jnp.float32)


def local(
    obs_own,
    obs_opp,
    actions,
    opponent_picks,
    policy_weight,
    policy_gain,
    action_table,
    value_gain,
    value_up,
    value_out,
):
    round_count = obs_own.shape[1]
    env_count = obs_own.shape[2]
    step_count = obs_own.shape[3]
    model_width = obs_own.shape[4]
    row_count = env_count * step_count
    weight_shard = policy_weight[0]
    own_gain = policy_gain[0]
    group_count = lax.axis_size("league")
    my_group = lax.axis_index("league")
    own_inputs = obs_own[0].reshape(round_count * row_count, model_width).astype(jnp.float32)
    own_normed = rms_norm(own_inputs, own_gain).astype(jnp.bfloat16)
    own_whole = lax.all_gather(weight_shard, "env", axis=0, tiled=True)
    own_state = own_inputs + jnp.dot(own_normed, own_whole, preferred_element_type=jnp.float32)
    every_pick = lax.all_gather(opponent_picks, "league", axis=0, tiled=True)
    action_range = jnp.arange(action_table.shape[0], dtype=jnp.int32)
    traj_list = []
    value_list = []
    for round_index in range(round_count):
        opp_raw = obs_opp[0, round_index].reshape(row_count, model_width)
        opp_inputs = opp_raw.astype(jnp.float32)
        all_rows = lax.all_gather(opp_raw, "league", axis=0, tiled=True)
        all_normed = rms_norm(all_rows.astype(jnp.float32), own_gain).astype(jnp.bfloat16)
        products = jnp.dot(all_normed, own_whole, preferred_element_type=jnp.float32)
        served = (every_pick[:, round_index] == my_group).astype(jnp.float32)
        products = (
            products.reshape(group_count, row_count, model_width) * served[:, None, None]
        ).astype(jnp.bfloat16)
        answers = lax.all_to_all(products, "league", split_axis=0, concat_axis=0, tiled=True)
        opp_state = opp_inputs + jnp.sum(answers.astype(jnp.float32), axis=0)
        own_ids = actions[0, 0, round_index].reshape(row_count)
        opp_ids = actions[0, 1, round_index].reshape(row_count)
        onehot = (own_ids[:, None] == action_range[None, :]).astype(jnp.bfloat16) + (
            opp_ids[:, None] == action_range[None, :]
        ).astype(jnp.bfloat16)
        action_sum = jnp.dot(onehot, action_table, preferred_element_type=jnp.float32)
        round_state = lax.dynamic_slice_in_dim(own_state, round_index * row_count, row_count, 0)
        joint_sum = round_state + opp_state + action_sum
        joint_row = rms_norm(joint_sum, value_gain).astype(jnp.bfloat16)
        value_hidden = jax.nn.silu(
            jnp.dot(joint_row, value_up, preferred_element_type=jnp.float32)
        ).astype(jnp.bfloat16)
        value_est = jnp.dot(value_hidden, value_out, preferred_element_type=jnp.float32)
        value_list.append(value_est.reshape(env_count, step_count))
        time_block = joint_row.reshape(env_count, step_count, model_width).transpose(1, 2, 0)
        traj_list.append(lax.all_to_all(time_block, "env", split_axis=1, concat_axis=2, tiled=True))
    learner_rows = jnp.stack(traj_list)
    values = jnp.stack(value_list)
    return (learner_rows[None], values[None])


def solution(mesh):
    in_specs = (
        P("league", None, "env", None, None),
        P("league", None, "env", None, None),
        P("league", None, None, "env", None),
        P("league", None),
        P("league", "env", None),
        P("league", None),
        P(),
        P(),
        P(),
        P(),
    )
    out_specs = (P("league", None, None, "env", None), P("league", None, "env", None))
    return jax.shard_map(local, mesh=mesh, in_specs=in_specs, out_specs=out_specs, check_vma=False)
```

profile of v0, /device:TPU:0, one launch (start us, length us, event | category | flops | bytes accessed | tf_op | source)
XLA Modules:
  0.0 430.5 jit_solution(11888221236370943280)
XLA Ops:
  7.2 0.0 copy-start
  7.2 0.0 all-gather.6.cloned.1.call-start
  7.2 3.2 fusion.43
  10.4 0.0 all-gather.6.cloned.1.call-update
  10.5 0.0 all-gather.10.cloned.1.call-start
  10.5 0.7 all-gather.10.cloned.1.call-update
  11.2 0.0 all-gather.8.cloned.1.call-start
  11.3 0.7 all-gather.8.cloned.1.call-update
  11.9 0.0 copy-done.14
  12.0 6.0 %all-gather.1 = s32[4,1,2]{2,1,0:T(1,128)S(1)} all-gather(s32[1,1,2]{2,1,0:T(1,128)S(1)} %bitcast.90), channel_id=1, replica_groups=mesh['league'=4,'env'=8] {'league'}, dimensions={0}, use_global_device_ids=true | all-gather | bytes 40 | tf_op jit(solution)/shard_map/all_gather | solution.py:37
  17.9 0.1 copy.23
  18.0 29.8 %all-gather.6.cloned.1.call-done = bf16[1024,2048]{1,0:T(8,128)(2,1)} async-done(((bf16[256,2048]{1,0:T(8,128)(2,1)}), bf16[1024,2048]{1,0:T(8,128)(2,1)}) %all-gather.6.cloned.1.call-update) | async-done | bytes 4194320 | tf_op jit(solution)/shard_map/all_gather | solution.py:44
  47.8 3.1 fusion
  50.9 124.0 %all-gather.10.cloned.1.call-done = bf16[1,2048,2048]{2,1,0:T(8,128)(2,1)} async-done(((bf16[1,256,2048]{2,1,0:T(8,128)(2,1)}), bf16[1,2048,2048]{2,1,0:T(8,128)(2,1)}) %all-gather.10.cloned.1.call-update) | async-done | bytes 8388624 | tf_op jit(solution)/shard_map/all_gather | solution.py:35
  174.9 12.6 %fusion.8 = f32[1024,2048]{1,0:T(8,128)S(1)} fusion(bf16[1,2048,2048]{2,1,0:T(8,128)(2,1)} %all-gather.10.cloned.1.call-done, bf16[1024,2048]{1,0:T(8,128)(2,1)} %all-gather.6.cloned.1.call-done, f32[2048]{0:T(1024)S(1)} %bitcast.84, f32[1024]{0:T(1024)S(1)} %add_rsqrt_fusion.2), kind=kOutput, calls=%fused_computation.12 | convolution fusion | flops 8598323200 | bytes 20983808 | tf_op jit(solution)/shard_map/dot_general | solution.py:46
  187.5 3.2 multiply_convert_fusion.1
  190.7 4.9 %all-to-all-start = ((bf16[4,256,2048]{2,1,0:T(8,128)(2,1)}), bf16[4,256,2048]{2,1,0:T(8,128)(2,1)}, u32[]{:S(2)}, u32[]{:S(2)}) async-start(bf16[4,256,2048]{2,1,0:T(8,128)(2,1)} %multiply_convert_fusion.1), calls=%async_computation | async-start | bytes 8388608 | tf_op jit(solution)/shard_map/all_to_all | solution.py:51
  195.6 22.4 %all-gather.8.cloned.1.call-done = bf16[1024,2048]{1,0:T(8,128)(2,1)} async-done(((bf16[256,2048]{1,0:T(8,128)(2,1)}), bf16[1024,2048]{1,0:T(8,128)(2,1)}) %all-gather.8.cloned.1.call-update) | async-done | bytes 4194320 | tf_op jit(solution)/shard_map/all_gather | solution.py:44
  218.0 3.2 fusion.3
  221.2 0.2 copy-done.7
  221.4 11.3 %fusion.6 = f32[1024,2048]{1,0:T(8,128)S(1)} fusion(bf16[1,2048,2048]{2,1,0:T(8,128)(2,1)} %all-gather.10.cloned.1.call-done, bf16[1024,2048]{1,0:T(8,128)(2,1)S(1)} %copy-done.7, f32[1024]{0:T(1024)S(1)} %add_rsqrt_fusion.1, f32[2048]{0:T(1024)S(1)} %bitcast.85), kind=kOutput, calls=%fused_computation.10 | convolution fusion | flops 8598323200 | bytes 20983808 | tf_op jit(solution)/shard_map/dot_general | solution.py:46
  232.7 3.2 multiply_convert_fusion
  235.9 16.6 %all-to-all-done = bf16[4,256,2048]{2,1,0:T(8,128)(2,1)} async-done(((bf16[4,256,2048]{2,1,0:T(8,128)(2,1)}), bf16[4,256,2048]{2,1,0:T(8,128)(2,1)}, u32[]{:S(2)}, u32[]{:S(2)}) %all-to-all-start) | async-done | bytes 4194336 | tf_op jit(solution)/shard_map/all_to_all | solution.py:51
  252.6 5.0 %all-to-all-start.2 = ((bf16[4,256,2048]{2,1,0:T(8,128)(2,1)}), bf16[4,256,2048]{2,1,0:T(8,128)(2,1)}, u32[]{:S(2)}, u32[]{:S(2)}) async-start(bf16[4,256,2048]{2,1,0:T(8,128)(2,1)} %multiply_convert_fusion), calls=%async_computation.2 | async-start | bytes 8388608 | tf_op jit(solution)/shard_map/all_to_all | solution.py:51
  257.6 0.0 copy-done.10
  257.6 0.1 eq.86
  257.7 0.1 eq.82
  257.8 0.5 fusion.14
  258.3 0.1 rsqrt.44
  258.4 0.1 eq.95
  258.5 0.1 eq.91
  258.6 0.5 fusion.16
  259.1 7.0 %bitcast_add_fusion = f32[512,2048]{1,0:T(8,128)S(1)} fusion(bf16[1,2,16,16,2048]{4,3,2,1,0:T(8,128)(2,1)S(1)} %copy-done.4, bf16[512,2048]{1,0:T(8,128)(2,1)S(1)} %fusion.16, bf16[1,2048,2048]{2,1,0:T(8,128)(2,1)} %all-gather.10.cloned.1.call-done), kind=kOutput, calls=%fused_computation.20 | convolution fusion | flops 4297064448 | bytes 16777216 | tf_op jit(solution)/shard_map/dot_general | solution.py:36
  266.1 0.0 copy-start.2
  266.1 4.8 %convert_reduce_fusion.1 = f32[256,2048]{1,0:T(8,128)S(1)} fusion(bf16[4,256,2048]{2,1,0:T(8,128)(2,1)} %all-to-all-done), kind=kLoop, calls=%fused_computation.18 | loop fusion | flops 3670016 | bytes 6291456 | tf_op jit(solution)/shard_map/reduce_sum | solution.py:52
  271.0 2.1 multiply_reduce_fusion.1
  273.1 32.6 %all-to-all-done.2 = bf16[4,256,2048]{2,1,0:T(8,128)(2,1)} async-done(((bf16[4,256,2048]{2,1,0:T(8,128)(2,1)}), bf16[4,256,2048]{2,1,0:T(8,128)(2,1)}, u32[]{:S(2)}, u32[]{:S(2)}) %all-to-all-start.2) | async-done | bytes 4194336 | tf_op jit(solution)/shard_map/all_to_all | solution.py:51
  305.7 3.4 convert_reduce_fusion
  309.1 0.0 copy-done.6
  309.1 0.8 multiply_reduce_fusion
  310.0 0.7 copy-done.3
  310.7 0.4 multiply_convert_fusion.3
  311.1 0.0 copy-start.9
  311.2 8.8 %copy.27 = bf16[16,16,2048]{0,1,2:T(8,128)(2,1)} copy(bf16[16,16,2048]{2,1,0:T(8,128)(2,1)S(1)} %bitcast.81) | data formatting | bytes 2097152 | tf_op jit(solution)/shard_map/reshape | solution.py:67
  320.0 7.5 %bitcast_bitcast_fusion = bf16[2048,16,16]{2,1,0:T(8,128)(2,1)} fusion(bf16[16,16,2048]{0,1,2:T(8,128)(2,1)} %copy.27), kind=kLoop, calls=%fused_computation.71 | loop fusion | bytes 2097152
  327.5 11.2 %reshape.109 = bf16[8,2,32768]{2,1,0:T(2,128)(2,1)} reshape(bf16[2048,16,16]{2,1,0:T(8,128)(2,1)} %bitcast_bitcast_fusion) | data formatting | bytes 2097152
  338.7 5.5 %all-to-all-start.3 = ((bf16[8,2,32768]{2,1,0:T(2,128)(2,1)}), bf16[8,2,32768]{2,1,0:T(2,128)(2,1)S(1)}, u32[]{:S(2)}, u32[]{:S(2)}) async-start(bf16[8,2,32768]{2,1,0:T(2,128)(2,1)} %reshape.109), calls=%async_computation.3 | async-start | bytes 2097152 | tf_op jit(solution)/shard_map/all_to_all | solution.py:68
  344.2 8.8 %copy.24 = bf16[16,16,2048]{0,1,2:T(8,128)(2,1)} copy(bf16[16,16,2048]{2,1,0:T(8,128)(2,1)S(1)} %bitcast.80) | data formatting | bytes 2097152 | tf_op jit(solution)/shard_map/reshape | solution.py:67
  353.1 7.5 %bitcast_bitcast_fusion.1 = bf16[2048,16,16]{2,1,0:T(8,128)(2,1)} fusion(bf16[16,16,2048]{0,1,2:T(8,128)(2,1)} %copy.24), kind=kLoop, calls=%fused_computation.72 | loop fusion | bytes 2097152
  360.5 11.2 %reshape.111 = bf16[8,2,32768]{2,1,0:T(2,128)(2,1)} reshape(bf16[2048,16,16]{2,1,0:T(8,128)(2,1)} %bitcast_bitcast_fusion.1) | data formatting | bytes 2097152
  371.8 0.0 all-to-all-done.3
  371.8 6.0 %all-to-all-start.1 = ((bf16[8,2,32768]{2,1,0:T(2,128)(2,1)}), bf16[8,2,32768]{2,1,0:T(2,128)(2,1)S(1)}, u32[]{:S(2)}, u32[]{:S(2)}) async-start(bf16[8,2,32768]{2,1,0:T(2,128)(2,1)} %reshape.111), calls=%async_computation.1 | async-start | bytes 2097152 | tf_op jit(solution)/shard_map/all_to_all | solution.py:68
  377.8 3.9 fusion.24
  381.7 0.1 stack_reshape.7
  381.8 4.0 fusion.23
  385.8 0.1 stack_reshape.6
  385.9 0.7 maximum_bitcast_fusion.1
  386.5 7.6 %reshape.110 = bf16[2048,16,16]{2,1,0:T(8,128)(2,1)} reshape(bf16[8,2,32768]{2,1,0:T(2,128)(2,1)S(1)} %all-to-all-done.3) | data formatting | bytes 2097152
  394.1 9.1 %copy.29 = bf16[16,256,8,16]{1,3,2,0:T(8,128)(2,1)} copy(bf16[16,256,8,16]{3,0,1,2:T(8,128)(2,1)} %bitcast.72) | data formatting | bytes 2097152 | tf_op jit(solution)/shard_map/all_to_all | solution.py:68
  403.2 0.0 all-to-all-done.1
  403.2 7.6 %reshape.112 = bf16[2048,16,16]{2,1,0:T(8,128)(2,1)} reshape(bf16[8,2,32768]{2,1,0:T(2,128)(2,1)S(1)} %all-to-all-done.1) | data formatting | bytes 2097152
  410.8 9.1 %copy.26 = bf16[16,256,8,16]{1,3,2,0:T(8,128)(2,1)} copy(bf16[16,256,8,16]{3,0,1,2:T(8,128)(2,1)} %bitcast.73) | data formatting | bytes 2097152 | tf_op jit(solution)/shard_map/all_to_all | solution.py:68
  419.9 1.7 maximum_bitcast_fusion
  421.6 2.4 copy.30
  (31 shorter events, 0.1 us)
Async XLA Ops:
  7.2 263.8 %copy-start = (bf16[256,2048]{1,0:T(8,128)(2,1)S(1)}, bf16[256,2048]{1,0:T(8,128)(2,1)}, u32[]{:S(2)}) copy-start(bf16[256,2048]{1,0:T(8,128)(2,1)} %param.16) | copy-start | bytes 3145732
  7.2 4.8 %copy-start.14 = (s32[1,2]{1,0:T(1,128)S(1)}, s32[1,2]{1,0:T(1,128)}, u32[]{:S(2)}) copy-start(s32[1,2]{1,0:T(1,128)} %param.13) | copy-start | bytes 28
  7.2 10.7 %copy-start.11 = (bf16[1,2048]{1,0:T(2,128)(2,1)S(1)}, bf16[1,2048]{1,0:T(2,128)(2,1)}, u32[]{:S(2)}) copy-start(bf16[1,2048]{1,0:T(2,128)(2,1)} %param.15) | copy-start | bytes 12292
  7.2 40.6 %all-gather.6.cloned.1.call-start = ((), (), s32[]{:S(2)}) async-start(), calls=%async_computation.4 | async-start | bytes 5242880 | tf_op jit(solution)/shard_map/all_gather | solution.py:44
  10.5 164.4 %all-gather.10.cloned.1.call-start = ((), (), s32[]{:S(2)}) async-start(), calls=%async_computation.6 | async-start | bytes 9437184 | tf_op jit(solution)/shard_map/all_gather | solution.py:35
  11.2 206.8 %all-gather.8.cloned.1.call-start = ((), (), s32[]{:S(2)}) async-start(), calls=%async_computation.5 | async-start | bytes 5242880 | tf_op jit(solution)/shard_map/all_gather | solution.py:44
  190.7 61.9 %all-to-all-start = ((bf16[4,256,2048]{2,1,0:T(8,128)(2,1)}), bf16[4,256,2048]{2,1,0:T(8,128)(2,1)}, u32[]{:S(2)}, u32[]{:S(2)}) async-start(bf16[4,256,2048]{2,1,0:T(8,128)(2,1)} %multiply_convert_fusion.1), calls=%async_computation | async-start | bytes 8388608 | tf_op jit(solution)/shard_map/all_to_all | solution.py:51
  218.0 3.4 copy-start.7
  235.9 21.7 %copy-start.10 = (s32[1,2,2,16,16]{4,3,2,1,0:T(8,128)S(1)}, s32[1,2,2,16,16]{4,3,2,1,0:T(8,128)}, u32[]{:S(2)}) copy-start(s32[1,2,2,16,16]{4,3,2,1,0:T(8,128)} %param.12) | copy-start | bytes 12292
  235.9 21.9 %copy-start.4 = (bf16[1,2,16,16,2048]{4,3,2,1,0:T(8,128)(2,1)S(1)}, bf16[1,2,16,16,2048]{4,3,2,1,0:T(8,128)(2,1)}, u32[]{:S(2)}) copy-start(bf16[1,2,16,16,2048]{4,3,2,1,0:T(8,128)(2,1)} %param.10) | copy-start | bytes 6291460
  235.9 22.4 %copy-start.12 = (bf16[2048]{0:T(1024)(128)(2,1)S(1)}, bf16[2048]{0:T(1024)(128)(2,1)}, u32[]{:S(2)}) copy-start(bf16[2048]{0:T(1024)(128)(2,1)} %param.17) | copy-start | bytes 12292
  252.6 53.1 %all-to-all-start.2 = ((bf16[4,256,2048]{2,1,0:T(8,128)(2,1)}), bf16[4,256,2048]{2,1,0:T(8,128)(2,1)}, u32[]{:S(2)}, u32[]{:S(2)}) async-start(bf16[4,256,2048]{2,1,0:T(8,128)(2,1)} %multiply_convert_fusion), calls=%async_computation.2 | async-start | bytes 8388608 | tf_op jit(solution)/shard_map/all_to_all | solution.py:51
  266.1 4.9 %copy-start.5 = (f32[512,2048]{1,0:T(8,128)}, f32[512,2048]{1,0:T(8,128)S(1)}, u32[]{:S(2)}) copy-start(f32[512,2048]{1,0:T(8,128)S(1)} %bitcast_add_fusion) | copy-start | bytes 12582916
  266.1 4.9 %copy-start.2 = (bf16[1,1,16,16,2048]{4,3,2,1,0:T(8,128)(2,1)S(1)}, bf16[1,1,16,16,2048]{4,3,2,1,0:T(8,128)(2,1)}, u32[]{:S(2)}) copy-start(bf16[1,1,16,16,2048]{4,3,2,1,0:T(8,128)(2,1)} %get-tuple-element.8) | copy-start | bytes 3145732
  273.1 36.0 %copy-start.1 = (bf16[1,1,16,16,2048]{4,3,2,1,0:T(8,128)(2,1)S(1)}, bf16[1,1,16,16,2048]{4,3,2,1,0:T(8,128)(2,1)}, u32[]{:S(2)}) copy-start(bf16[1,1,16,16,2048]{4,3,2,1,0:T(8,128)(2,1)} %get-tuple-element.9) | copy-start | bytes 3145732
  305.7 3.4 copy-start.6
  309.1 1.6 copy-start.3
  311.1 8.8 %copy-start.9 = (bf16[256,2048]{1,0:T(8,128)(2,1)}, bf16[256,2048]{1,0:T(8,128)(2,1)S(1)}, u32[]{:S(2)}) copy-start(bf16[256,2048]{1,0:T(8,128)(2,1)S(1)} %get-tuple-element.15) | copy-start | bytes 3145732
  311.2 33.1 %copy-start.8 = (bf16[256,2048]{1,0:T(8,128)(2,1)}, bf16[256,2048]{1,0:T(8,128)(2,1)S(1)}, u32[]{:S(2)}) copy-start(bf16[256,2048]{1,0:T(8,128)(2,1)S(1)} %get-tuple-element.14) | copy-start | bytes 3145732
  338.7 33.1 %all-to-all-start.3 = ((bf16[8,2,32768]{2,1,0:T(2,128)(2,1)}), bf16[8,2,32768]{2,1,0:T(2,128)(2,1)S(1)}, u32[]{:S(2)}, u32[]{:S(2)}) async-start(bf16[8,2,32768]{2,1,0:T(2,128)(2,1)} %reshape.109), calls=%async_computation.3 | async-start | bytes 2097152 | tf_op jit(solution)/shard_map/all_to_all | solution.py:68
  360.5 17.2 %copy-start.13 = (bf16[1024]{0:T(1024)(128)(2,1)S(1)}, bf16[1024]{0:T(1024)(128)(2,1)}, u32[]{:S(2)}) copy-start(bf16[1024]{0:T(1024)(128)(2,1)} %param.19) | copy-start | bytes 6148
  371.8 31.4 %all-to-all-start.1 = ((bf16[8,2,32768]{2,1,0:T(2,128)(2,1)}), bf16[8,2,32768]{2,1,0:T(2,128)(2,1)S(1)}, u32[]{:S(2)}, u32[]{:S(2)}) async-start(bf16[8,2,32768]{2,1,0:T(2,128)(2,1)} %reshape.111), calls=%async_computation.1 | async-start | bytes 2097152 | tf_op jit(solution)/shard_map/all_to_all | solution.py:68
Sparse Core Ops, SparseCore 0:
  10.6 37.1 all-gather.5
  49.9 124.9 all-gather.9
  176.5 41.4 all-gather.7
where the time goes:
time: 432 us; the launch traced here: 431 us
  waiting for transfers between devices  227 us (53%)
  local copies, waits for them, and re-layouts  95.7 us (22%)
  matrix products  41.7 us (10%)
  other arithmetic  24.9 us (6%)
  starting transfers between devices  21.6 us (5%)
  between operations  14 us (3%)
  blocking collectives  5.95 us (1%)
    all_gather x1, waiting for transfers between devices, local(): own_whole = lax.all_gather(weight_shard, 'env', axis=0, tiled=True)  124 us
    unnamed x38, local copies, waits for them, and re-layouts  56 us
    all_gather x2, waiting for transfers between devices, local(): all_rows = lax.all_gather(opp_raw, 'league', axis=0, tiled=True)  52.1 us
    all_to_all x2, waiting for transfers between devices, local(): lax.all_to_all(products, 'league', split_axis=0, concat_axis=0, tiled=True)  49.2 us
    dot_general x2, matrix products, local(): jnp.dot(all_normed, own_whole, preferred_element_type=jnp.float32)  23.9 us
    all_to_all x2, local copies, waits for them, and re-layouts, local(): lax.all_to_all(time_block, 'env', split_axis=1, concat_axis=2, tiled=True)  18.2 us
    reshape x2, local copies, waits for them, and re-layouts, local(): joint_row.reshape(env_count, step_count, model_width).transpose(1, 2, 0)  17.7 us
    all_to_all x2, starting transfers between devices, local(): lax.all_to_all(time_block, 'env', split_axis=1, concat_axis=2, tiled=True)  11.5 us
  transfers between devices with their start and end apart: 7, of which 5 were waited for; matrix products, arithmetic and copies ran while one was open for 24% of the time, Pallas kernels for 0%

commit v1 on v0

--- a/solution.py
+++ b/solution.py
@@ -41,7 +41,26 @@
     for round_index in range(round_count):
         opp_raw = obs_opp[0, round_index].reshape(row_count, model_width)
         opp_inputs = opp_raw.astype(jnp.float32)
-        all_rows = lax.all_gather(opp_raw, "league", axis=0, tiled=True)
+        size, position, rows = (lax.axis_size("league"), lax.axis_index("league"), opp_raw.shape[0])
+        ahead = [(i, (i + 1) % size) for i in range(size)]
+        left = [(i, (i - 1) % size) for i in range(size)]
+        filled = jnp.zeros(
+            (*opp_raw.shape[:0], size * rows, *opp_raw.shape[0 + 1 :]), opp_raw.dtype
+        )
+        filled = lax.dynamic_update_slice_in_dim(filled, opp_raw, position * rows, axis=0)
+        from_left = from_right = opp_raw
+        halfway = size // 2
+        for step in range(1, halfway + 1):
+            from_left = lax.ppermute(from_left, "league", ahead)
+            filled = lax.dynamic_update_slice_in_dim(
+                filled, from_left, (position - step) % size * rows, axis=0
+            )
+            if step < size - halfway:
+                from_right = lax.ppermute(from_right, "league", left)
+                filled = lax.dynamic_update_slice_in_dim(
+                    filled, from_right, (position + step) % size * rows, axis=0
+                )
+        all_rows = filled
         all_normed = rms_norm(all_rows.astype(jnp.float32), own_gain).astype(jnp.bfloat16)
         products = jnp.dot(all_normed, own_whole, preferred_element_type=jnp.float32)
         served = (every_pick[:, round_index] == my_group).astype(jnp.float32)

time: 432 us -> 385 us (0.89)
  waiting for transfers between devices: 227 us -> 123 us
  blocking collectives: 5.95 us -> 41.4 us
  local copies, waits for them, and re-layouts: 95.7 us -> 111 us
    all_gather x1, waiting for transfers between devices: 124 us -> 46.3 us  [local(): own_whole = lax.all_gather(weight_shard, 'env', axis=0, tiled=True)]
    all_gather x2 -> x0, waiting for transfers between devices: 52.1 us -> none  [local(): all_rows = lax.all_gather(opp_raw, 'league', axis=0, tiled=True)]
    all_gather x1, blocking collectives: 5.95 us -> 41.4 us  [local(): every_pick = lax.all_gather(opponent_picks, 'league', axis=0, tiled=True)]
    ppermute x0 -> x6, waiting for transfers between devices: none -> 14.2 us  [the longest x4 14.2 us: local(): from_left = lax.ppermute(from_left, 'league', ahead)]
    dynamic_update_slice x0 -> x7, local copies, waits for them, and re-layouts: none -> 13.9 us  [the longest x3 8.06 us: local(): lax.dynamic_update_slice_in_dim(filled, from_left, (position - step) % si...]
    all_to_all x2, waiting for transfers between devices: 49.2 us -> 61.6 us  [local(): lax.all_to_all(products, 'league', split_axis=0, concat_axis=0, tiled=True)]
    ppermute x0 -> x6, starting transfers between devices: none -> 5.65 us  [the longest x4 5.52 us: local(): from_left = lax.ppermute(from_left, 'league', ahead)]
  transfers between devices with their start and end apart: 7 -> 11, of which waited for: 5 -> 6; matrix products, arithmetic and copies ran while one was open for 24% -> 29% of each run, Pallas kernels for 0% -> 0%
where the time goes in v1:
time: 385 us; the launch traced here: 383 us
  waiting for transfers between devices  123 us (32%)
  local copies, waits for them, and re-layouts  111 us (29%)
  matrix products  41.7 us (11%)
  blocking collectives  41.4 us (11%)
  other arithmetic  26.4 us (7%)
  starting transfers between devices  25.3 us (7%)
  between operations  14.3 us (4%)
    all_to_all x2, waiting for transfers between devices, local(): lax.all_to_all(products, 'league', split_axis=0, concat_axis=0, tiled=True)  61.6 us
    unnamed x38, local copies, waits for them, and re-layouts  56 us
    all_gather x1, waiting for transfers between devices, local(): own_whole = lax.all_gather(weight_shard, 'env', axis=0, tiled=True)  46.3 us
    all_gather x1, blocking collectives, local(): every_pick = lax.all_gather(opponent_picks, 'league', axis=0, tiled=True)  41.4 us
    dot_general x2, matrix products, local(): jnp.dot(all_normed, own_whole, preferred_element_type=jnp.float32)  23.9 us
    all_to_all x2, local copies, waits for them, and re-layouts, local(): lax.all_to_all(time_block, 'env', split_axis=1, concat_axis=2, tiled=True)  18.2 us
    reshape x2, local copies, waits for them, and re-layouts, local(): joint_row.reshape(env_count, step_count, model_width).transpose(1, 2, 0)  17.7 us
    ppermute x4, waiting for transfers between devices, local(): from_left = lax.ppermute(from_left, 'league', ahead)  14.2 us
  transfers between devices with their start and end apart: 11, of which 6 were waited for; matrix products, arithmetic and copies ran while one was open for 29% of the time, Pallas kernels for 0%

profile of v1, /device:TPU:0, one launch (start us, length us, event | category | flops | bytes accessed | tf_op | source)
XLA Modules:
  0.0 383.1 jit_solution(6959375198091400153)
XLA Ops:
  7.2 0.7 all-gather.4.cloned.1.call-update
  7.9 1.7 fusion.43
  9.6 0.5 collective-permute-start
  10.1 2.6 collective-permute-start.3
  12.7 0.1 collective-permute-start.4
  12.8 0.5 broadcast.92.clone.1
  13.4 0.1 constant_dynamic-update-slice_fusion.7
  13.5 2.5 broadcast.92.clone
  16.0 1.1 constant_dynamic-update-slice_fusion.3
  17.1 0.5 fusion.14
  17.6 41.4 %all-gather.1 = s32[4,1,2]{2,1,0:T(1,128)S(1)} all-gather(s32[1,1,2]{2,1,0:T(1,128)S(1)} %bitcast.94), channel_id=1, replica_groups=mesh['league'=4,'env'=8] {'league'}, dimensions={0}, use_global_device_ids=true | all-gather | bytes 40 | tf_op jit(solution)/shard_map/all_gather | solution.py:37
  59.0 0.1 copy.23
  59.1 0.3 collective-permute-start.2
  59.4 2.1 collective-permute-start.5
  61.6 2.3 constant_dynamic-update-slice_fusion.6
  63.9 2.6 constant_dynamic-update-slice_fusion.2
  66.5 2.3 constant_dynamic-update-slice_fusion.5
  68.8 2.3 constant_dynamic-update-slice_fusion.1
  71.2 2.9 collective-permute-done.2
  74.1 11.2 %collective-permute-done.5 = bf16[256,2048]{1,0:T(8,128)(2,1)} collective-permute-done((bf16[256,2048]{1,0:T(8,128)(2,1)}, bf16[256,2048]{1,0:T(8,128)(2,1)}, u32[]{:S(2)}, u32[]{:S(2)}) %collective-permute-start.5) | collective-permute-done | bytes 1048608 | tf_op jit(solution)/shard_map/ppermute | solution.py:54
  85.4 3.1 constant_dynamic-update-slice_fusion
  88.4 3.1 fusion.3
  91.6 46.3 %all-gather.4.cloned.1.call-done = bf16[1,2048,2048]{2,1,0:T(8,128)(2,1)} async-done(((bf16[1,256,2048]{2,1,0:T(8,128)(2,1)}), bf16[1,2048,2048]{2,1,0:T(8,128)(2,1)}) %all-gather.4.cloned.1.call-update) | async-done | bytes 8388624 | tf_op jit(solution)/shard_map/all_gather | solution.py:35
  137.8 12.6 %fusion.6 = f32[1024,2048]{1,0:T(8,128)S(1)} fusion(bf16[1,2048,2048]{2,1,0:T(8,128)(2,1)} %all-gather.4.cloned.1.call-done, bf16[1024,2048]{1,0:T(8,128)(2,1)} %get-tuple-element.22, f32[1024]{0:T(1024)S(1)} %add_rsqrt_fusion.1, f32[2048]{0:T(1024)S(1)} %bitcast.88), kind=kOutput, calls=%fused_computation.10 | convolution fusion | flops 8598323200 | bytes 20983808 | tf_op jit(solution)/shard_map/dot_general | solution.py:65
  150.4 3.2 multiply_convert_fusion
  153.6 5.1 %all-to-all-start.2 = ((bf16[4,256,2048]{2,1,0:T(8,128)(2,1)}), bf16[4,256,2048]{2,1,0:T(8,128)(2,1)}, u32[]{:S(2)}, u32[]{:S(2)}) async-start(bf16[4,256,2048]{2,1,0:T(8,128)(2,1)} %multiply_convert_fusion), calls=%async_computation.2 | async-start | bytes 8388608 | tf_op jit(solution)/shard_map/all_to_all | solution.py:70
  158.7 3.2 fusion
  162.0 0.2 copy-done.2
  162.2 11.3 %fusion.8 = f32[1024,2048]{1,0:T(8,128)S(1)} fusion(bf16[1,2048,2048]{2,1,0:T(8,128)(2,1)} %all-gather.4.cloned.1.call-done, bf16[1024,2048]{1,0:T(8,128)(2,1)S(1)} %copy-done.2, f32[2048]{0:T(1024)S(1)} %bitcast.89, f32[1024]{0:T(1024)S(1)} %add_rsqrt_fusion.2), kind=kOutput, calls=%fused_computation.12 | convolution fusion | flops 8598323200 | bytes 20983808 | tf_op jit(solution)/shard_map/dot_general | solution.py:65
  173.5 3.2 multiply_convert_fusion.1
  176.7 30.1 %all-to-all-done.2 = bf16[4,256,2048]{2,1,0:T(8,128)(2,1)} async-done(((bf16[4,256,2048]{2,1,0:T(8,128)(2,1)}), bf16[4,256,2048]{2,1,0:T(8,128)(2,1)}, u32[]{:S(2)}, u32[]{:S(2)}) %all-to-all-start.2) | async-done | bytes 4194336 | tf_op jit(solution)/shard_map/all_to_all | solution.py:70
  206.8 5.1 %all-to-all-start = ((bf16[4,256,2048]{2,1,0:T(8,128)(2,1)}), bf16[4,256,2048]{2,1,0:T(8,128)(2,1)}, u32[]{:S(2)}, u32[]{:S(2)}) async-start(bf16[4,256,2048]{2,1,0:T(8,128)(2,1)} %multiply_convert_fusion.1), calls=%async_computation | async-start | bytes 8388608 | tf_op jit(solution)/shard_map/all_to_all | solution.py:70
  211.9 0.1 rsqrt.44
  212.0 0.1 eq.102
  212.0 0.1 eq.98
  212.1 0.1 eq.89
  212.2 0.1 eq.93
  212.3 2.3 fusion.16
  214.6 7.0 %bitcast_add_fusion = f32[512,2048]{1,0:T(8,128)S(1)} fusion(bf16[1,2,16,16,2048]{4,3,2,1,0:T(8,128)(2,1)S(1)} %copy-done.5, bf16[512,2048]{1,0:T(8,128)(2,1)S(1)} %fusion.16, bf16[1,2048,2048]{2,1,0:T(8,128)(2,1)} %all-gather.4.cloned.1.call-done), kind=kOutput, calls=%fused_computation.20 | convolution fusion | flops 4297064448 | bytes 16777216 | tf_op jit(solution)/shard_map/dot_general | solution.py:36
  221.6 4.6 %convert_reduce_fusion = f32[256,2048]{1,0:T(8,128)S(1)} fusion(bf16[4,256,2048]{2,1,0:T(8,128)(2,1)} %all-to-all-done.2), kind=kLoop, calls=%fused_computation.16 | loop fusion | flops 3670016 | bytes 6291456 | tf_op jit(solution)/shard_map/reduce_sum | solution.py:71
  226.2 2.1 multiply_reduce_fusion
  228.3 31.5 %all-to-all-done = bf16[4,256,2048]{2,1,0:T(8,128)(2,1)} async-done(((bf16[4,256,2048]{2,1,0:T(8,128)(2,1)}), bf16[4,256,2048]{2,1,0:T(8,128)(2,1)}, u32[]{:S(2)}, u32[]{:S(2)}) %all-to-all-start) | async-done | bytes 4194336 | tf_op jit(solution)/shard_map/all_to_all | solution.py:70
  259.9 3.4 convert_reduce_fusion.1
  263.3 0.8 multiply_reduce_fusion.1
  264.2 0.7 copy-done.3
  264.9 0.4 multiply_convert_fusion.3
  265.3 8.8 %copy.24 = bf16[16,16,2048]{0,1,2:T(8,128)(2,1)} copy(bf16[16,16,2048]{2,1,0:T(8,128)(2,1)S(1)} %bitcast.85) | data formatting | bytes 2097152 | tf_op jit(solution)/shard_map/reshape | solution.py:86
  274.2 7.5 %bitcast_bitcast_fusion.1 = bf16[2048,16,16]{2,1,0:T(8,128)(2,1)} fusion(bf16[16,16,2048]{0,1,2:T(8,128)(2,1)} %copy.24), kind=kLoop, calls=%fused_computation.80 | loop fusion | bytes 2097152
  281.6 11.2 %reshape.111 = bf16[8,2,32768]{2,1,0:T(2,128)(2,1)} reshape(bf16[2048,16,16]{2,1,0:T(8,128)(2,1)} %bitcast_bitcast_fusion.1) | data formatting | bytes 2097152
  292.9 3.6 all-to-all-start.1
  296.5 8.8 %copy.27 = bf16[16,16,2048]{0,1,2:T(8,128)(2,1)} copy(bf16[16,16,2048]{2,1,0:T(8,128)(2,1)S(1)} %bitcast.84) | data formatting | bytes 2097152 | tf_op jit(solution)/shard_map/reshape | solution.py:86
  305.3 7.5 %bitcast_bitcast_fusion = bf16[2048,16,16]{2,1,0:T(8,128)(2,1)} fusion(bf16[16,16,2048]{0,1,2:T(8,128)(2,1)} %copy.27), kind=kLoop, calls=%fused_computation.79 | loop fusion | bytes 2097152
  312.8 11.3 %reshape.109 = bf16[8,2,32768]{2,1,0:T(2,128)(2,1)} reshape(bf16[2048,16,16]{2,1,0:T(8,128)(2,1)} %bitcast_bitcast_fusion) | data formatting | bytes 2097152
  324.0 5.9 %all-to-all-start.3 = ((bf16[8,2,32768]{2,1,0:T(2,128)(2,1)}), bf16[8,2,32768]{2,1,0:T(2,128)(2,1)S(1)}, u32[]{:S(2)}, u32[]{:S(2)}) async-start(bf16[8,2,32768]{2,1,0:T(2,128)(2,1)} %reshape.109), calls=%async_computation.3 | async-start | bytes 2097152 | tf_op jit(solution)/shard_map/all_to_all | solution.py:87
  330.0 3.9 %fusion.23 = f32[1,256]{1,0:T(1,128)S(1)} fusion(bf16[1024,1]{0,1:T(2,128)(2,1)S(1)} %reshape.105, bf16[256,2048]{1,0:T(8,128)(2,1)} %copy-done.9, bf16[2048,1024]{1,0:T(8,128)(2,1)} %param.18), kind=kOutput, calls=%fused_computation.41 | convolution fusion | flops 1075576832 | bytes 5245952 | tf_op jit(solution)/shard_map/dot_general | solution.py:84
  333.9 0.1 stack_reshape.6
  334.0 4.0 %fusion.24 = f32[1,256]{1,0:T(1,128)S(1)} fusion(bf16[1024,1]{0,1:T(2,128)(2,1)S(1)} %reshape.105, bf16[256,2048]{1,0:T(8,128)(2,1)} %copy-done.8, bf16[2048,1024]{1,0:T(8,128)(2,1)} %param.18), kind=kOutput, calls=%fused_computation.42 | convolution fusion | flops 1075576832 | bytes 5245952 | tf_op jit(solution)/shard_map/dot_general | solution.py:84
  338.0 0.7 maximum_bitcast_fusion.1
  338.7 7.6 %reshape.112 = bf16[2048,16,16]{2,1,0:T(8,128)(2,1)} reshape(bf16[8,2,32768]{2,1,0:T(2,128)(2,1)S(1)} %all-to-all-done.1) | data formatting | bytes 2097152
  346.3 9.1 %copy.26 = bf16[16,256,8,16]{1,3,2,0:T(8,128)(2,1)} copy(bf16[16,256,8,16]{3,0,1,2:T(8,128)(2,1)} %bitcast.72) | data formatting | bytes 2097152 | tf_op jit(solution)/shard_map/all_to_all | solution.py:87
  355.4 7.6 %reshape.110 = bf16[2048,16,16]{2,1,0:T(8,128)(2,1)} reshape(bf16[8,2,32768]{2,1,0:T(2,128)(2,1)S(1)} %all-to-all-done.3) | data formatting | bytes 2097152
  363.0 9.1 %copy.29 = bf16[16,256,8,16]{1,3,2,0:T(8,128)(2,1)} copy(bf16[16,256,8,16]{3,0,1,2:T(8,128)(2,1)} %bitcast.73) | data formatting | bytes 2097152 | tf_op jit(solution)/shard_map/all_to_all | solution.py:87
  372.1 1.7 maximum_bitcast_fusion
  373.8 2.4 copy.30
  (47 shorter events, 0.4 us)
Async XLA Ops:
  7.2 219.1 %copy-start = (bf16[256,2048]{1,0:T(8,128)(2,1)S(1)}, bf16[256,2048]{1,0:T(8,128)(2,1)}, u32[]{:S(2)}) copy-start(bf16[256,2048]{1,0:T(8,128)(2,1)} %param.16) | copy-start | bytes 3145732
  7.2 130.6 %all-gather.4.cloned.1.call-start = ((), (), s32[]{:S(2)}) async-start(), calls=%async_computation.4 | async-start | bytes 9437184 | tf_op jit(solution)/shard_map/all_gather | solution.py:35
  9.6 49.5 %collective-permute-start = (bf16[256,2048]{1,0:T(8,128)(2,1)S(1)}, bf16[256,2048]{1,0:T(8,128)(2,1)}, u32[]{:S(2)}, u32[]{:S(2)}) collective-permute-start(bf16[256,2048]{1,0:T(8,128)(2,1)S(1)} %bitcast.74), channel_id=1, source_target_pairs={{0,8},{8,16},{16,24},{24,0},{1,9},{9,17},{17,25},{25,1},{2,10},{10... | collective-permute-start | bytes 3145736 | tf_op jit(solution)/shard_map/ppermute | solution.py:54
  10.1 49.3 %collective-permute-start.3 = (bf16[256,2048]{1,0:T(8,128)(2,1)S(1)}, bf16[256,2048]{1,0:T(8,128)(2,1)}, u32[]{:S(2)}, u32[]{:S(2)}) collective-permute-start(bf16[256,2048]{1,0:T(8,128)(2,1)S(1)} %bitcast.78), channel_id=1, source_target_pairs={{0,8},{8,16},{16,24},{24,0},{1,9},{9,17},{17,25},{25,1},{2,10},{10... | collective-permute-start | bytes 3145736 | tf_op jit(solution)/shard_map/ppermute | solution.py:54
  12.7 53.8 %collective-permute-start.1 = (bf16[256,2048]{1,0:T(8,128)(2,1)S(1)}, bf16[256,2048]{1,0:T(8,128)(2,1)}, u32[]{:S(2)}, u32[]{:S(2)}) collective-permute-start(bf16[256,2048]{1,0:T(8,128)(2,1)S(1)} %bitcast.75), channel_id=1, source_target_pairs={{0,24},{8,0},{16,8},{24,16},{1,25},{9,1},{17,9},{25,17},{2,26},{10... | collective-permute-start | bytes 3145736 | tf_op jit(solution)/shard_map/ppermute | solution.py:59
  12.7 56.1 %collective-permute-start.4 = (bf16[256,2048]{1,0:T(8,128)(2,1)S(1)}, bf16[256,2048]{1,0:T(8,128)(2,1)}, u32[]{:S(2)}, u32[]{:S(2)}) collective-permute-start(bf16[256,2048]{1,0:T(8,128)(2,1)S(1)} %bitcast.79), channel_id=1, source_target_pairs={{0,24},{8,0},{16,8},{24,16},{1,25},{9,1},{17,9},{25,17},{2,26},{10... | collective-permute-start | bytes 3145736 | tf_op jit(solution)/shard_map/ppermute | solution.py:59
  13.4 3.8 copy-start.4
  13.5 4.1 %copy-start.1 = (bf16[1024,2048]{1,0:T(8,128)(2,1)}, bf16[1024,2048]{1,0:T(8,128)(2,1)S(1)}, u32[]{:S(2)}) copy-start(bf16[1024,2048]{1,0:T(8,128)(2,1)S(1)} %constant_dynamic-update-slice_fusion.7) | copy-start | bytes 12582916
  13.5 4.1 %copy-start.14 = (s32[1,2]{1,0:T(1,128)S(1)}, s32[1,2]{1,0:T(1,128)}, u32[]{:S(2)}) copy-start(s32[1,2]{1,0:T(1,128)} %param.13) | copy-start | bytes 28
  13.5 48.0 %copy-start.11 = (bf16[1,2048]{1,0:T(2,128)(2,1)S(1)}, bf16[1,2048]{1,0:T(2,128)(2,1)}, u32[]{:S(2)}) copy-start(bf16[1,2048]{1,0:T(2,128)(2,1)} %param.15) | copy-start | bytes 12292
  59.1 15.0 %collective-permute-start.2 = (bf16[256,2048]{1,0:T(8,128)(2,1)}, bf16[256,2048]{1,0:T(8,128)(2,1)}, u32[]{:S(2)}, u32[]{:S(2)}) collective-permute-start(bf16[256,2048]{1,0:T(8,128)(2,1)} %collective-permute-done), channel_id=1, source_target_pairs={{0,8},{8,16},{16,24},{24,0},{1,9},{9,17},{17,25},{25,1},{2,10},{10... | collective-permute-start | bytes 3145736 | tf_op jit(solution)/shard_map/ppermute | solution.py:54
  59.4 25.9 %collective-permute-start.5 = (bf16[256,2048]{1,0:T(8,128)(2,1)}, bf16[256,2048]{1,0:T(8,128)(2,1)}, u32[]{:S(2)}, u32[]{:S(2)}) collective-permute-start(bf16[256,2048]{1,0:T(8,128)(2,1)} %collective-permute-done.3), channel_id=1, source_target_pairs={{0,8},{8,16},{16,24},{24,0},{1,9},{9,17},{17,25},{25,1},{2,10},{10... | collective-permute-start | bytes 3145736 | tf_op jit(solution)/shard_map/ppermute | solution.py:54
  153.6 53.2 %all-to-all-start.2 = ((bf16[4,256,2048]{2,1,0:T(8,128)(2,1)}), bf16[4,256,2048]{2,1,0:T(8,128)(2,1)}, u32[]{:S(2)}, u32[]{:S(2)}) async-start(bf16[4,256,2048]{2,1,0:T(8,128)(2,1)} %multiply_convert_fusion), calls=%async_computation.2 | async-start | bytes 8388608 | tf_op jit(solution)/shard_map/all_to_all | solution.py:70
  158.7 3.5 copy-start.2
  176.7 35.3 %copy-start.10 = (s32[1,2,2,16,16]{4,3,2,1,0:T(8,128)S(1)}, s32[1,2,2,16,16]{4,3,2,1,0:T(8,128)}, u32[]{:S(2)}) copy-start(s32[1,2,2,16,16]{4,3,2,1,0:T(8,128)} %param.12) | copy-start | bytes 12292
  176.7 35.6 %copy-start.12 = (bf16[2048]{0:T(1024)(128)(2,1)S(1)}, bf16[2048]{0:T(1024)(128)(2,1)}, u32[]{:S(2)}) copy-start(bf16[2048]{0:T(1024)(128)(2,1)} %param.17) | copy-start | bytes 12292
  206.8 53.1 %all-to-all-start = ((bf16[4,256,2048]{2,1,0:T(8,128)(2,1)}), bf16[4,256,2048]{2,1,0:T(8,128)(2,1)}, u32[]{:S(2)}, u32[]{:S(2)}) async-start(bf16[4,256,2048]{2,1,0:T(8,128)(2,1)} %multiply_convert_fusion.1), calls=%async_computation | async-start | bytes 8388608 | tf_op jit(solution)/shard_map/all_to_all | solution.py:70
  212.3 2.3 copy-start.5
  221.6 6.7 %copy-start.6 = (f32[512,2048]{1,0:T(8,128)}, f32[512,2048]{1,0:T(8,128)S(1)}, u32[]{:S(2)}) copy-start(f32[512,2048]{1,0:T(8,128)S(1)} %bitcast_add_fusion) | copy-start | bytes 12582916
  259.9 3.4 copy-start.7
  263.3 1.6 copy-start.3
  265.3 8.8 %copy-start.9 = (bf16[256,2048]{1,0:T(8,128)(2,1)}, bf16[256,2048]{1,0:T(8,128)(2,1)S(1)}, u32[]{:S(2)}) copy-start(bf16[256,2048]{1,0:T(8,128)(2,1)S(1)} %get-tuple-element.14) | copy-start | bytes 3145732
  265.3 31.1 %copy-start.8 = (bf16[256,2048]{1,0:T(8,128)(2,1)}, bf16[256,2048]{1,0:T(8,128)(2,1)S(1)}, u32[]{:S(2)}) copy-start(bf16[256,2048]{1,0:T(8,128)(2,1)S(1)} %get-tuple-element.15) | copy-start | bytes 3145732
  292.9 31.1 %all-to-all-start.1 = ((bf16[8,2,32768]{2,1,0:T(2,128)(2,1)}), bf16[8,2,32768]{2,1,0:T(2,128)(2,1)S(1)}, u32[]{:S(2)}, u32[]{:S(2)}) async-start(bf16[8,2,32768]{2,1,0:T(2,128)(2,1)} %reshape.111), calls=%async_computation.1 | async-start | bytes 2097152 | tf_op jit(solution)/shard_map/all_to_all | solution.py:87
  312.8 17.2 %copy-start.13 = (bf16[1024]{0:T(1024)(128)(2,1)S(1)}, bf16[1024]{0:T(1024)(128)(2,1)}, u32[]{:S(2)}) copy-start(bf16[1024]{0:T(1024)(128)(2,1)} %param.19) | copy-start | bytes 6148
  324.0 31.4 %all-to-all-start.3 = ((bf16[8,2,32768]{2,1,0:T(2,128)(2,1)}), bf16[8,2,32768]{2,1,0:T(2,128)(2,1)S(1)}, u32[]{:S(2)}, u32[]{:S(2)}) async-start(bf16[8,2,32768]{2,1,0:T(2,128)(2,1)} %reshape.109), calls=%async_computation.3 | async-start | bytes 2097152 | tf_op jit(solution)/shard_map/all_to_all | solution.py:87
Sparse Core Ops, SparseCore 0:
  10.1 127.6 all-gather.3
